TPU v7x, 256 devices: a whole 4x4x8 slice. The times are simulated.
256 devices in a mesh: node: 64 (over z, x, core), site: 4 (over y).
Axes of the slice: x: 4, y: 4, z: 8, core: 2. Of those that a mesh axis runs over, the one named last changes fastest.
Arguments:
- leaf_partials: float32 [4096, 4, 4096], P('node', None, 'site'), may hold values from 0.05 to 1
- dag_edges: int32 [3, 12288, 3], P(None, 'node'), may hold values from 0 to 4095, as said below
- weights: float32 [3, 12288], P(None, 'node'), may hold values from 0.25 to 4
- lengths: float32 [3, 12288], P(None, 'node'), may hold values from 0.02 to 2
- counts: int32 [4096], P('site'), may hold values from 1 to 9
- topo_nodes: int32 [256, 8], P('node'), may hold values from 0 to 4095
Outputs:
- topology_loglik: float32 [256], P('node')
- edge_gradient: float32 [12288], P('node')
Inputs may be any that keep to these rules, and one draw needn't show every extreme that they name: `dag_edges`: in every level each subsplit is the child of exactly 3 edges, listed on the index of node that owns the child; subsplit n is owned by index n // 64. Column 1 is the parent in the next level, column 2 the rotation (0 or 1). Every parent has at least one edge of each rotation. Among the edges of one index of node, at most 4 have parents owned by any one index, and some index receives exactly 4 from every index.
All inputs are finite; a program needn't handle non-finite values.
Results may differ from a plain program's by a relative error of at most 0.0003.
Values sent between devices are 32-bit elements; how exact they have to be, the bound alone decides.
No kernel may reach another device: no remote copies, remote signals or barrier semaphores. Data moves between devices by JAX's collectives and lax.ppermute only.
A program may use at most 192 MiB of HBM per device.

v0:
```python
import jax
import jax.numpy as jnp
from jax import lax
from jax.sharding import PartitionSpec as P


def transit(child_rows, branch):
    survival = jnp.exp(branch * (-4.0 / 3.0))[:, None, None]
    return survival * child_rows + (1.0 - survival) * 0.25 * jnp.sum(
        child_rows, axis=1, keepdims=True
    )


def on_device(leaf_partials, dag_edges, weights, lengths, counts, topo_nodes):
    node_dev, states, site_dev = leaf_partials.shape
    level_count, edge_dev = (dag_edges.shape[0], dag_edges.shape[1])
    owners = lax.axis_size("node")
    device = lax.axis_index("node")
    nodes_all = node_dev * owners
    sites_all = site_dev * lax.axis_size("site")
    scaled = counts.astype(jnp.float32) / sites_all
    incidence = lax.all_gather(topo_nodes, "node", axis=0, tiled=True)
    multiplicity = jax.ops.segment_sum(
        jnp.ones((incidence.size,), jnp.float32), incidence.reshape(-1), num_segments=nodes_all
    )
    capacity = 4 * node_dev // owners
    slots_all = owners * capacity
    current = leaf_partials
    for level_index in range(level_count):
        child_index = dag_edges[level_index, :, 0] - device * node_dev
        parents = dag_edges[level_index, :, 1]
        rotation = dag_edges[level_index, :, 2]
        message = transit(current[child_index], lengths[level_index])
        owner_dev = parents // node_dev
        one_hot = (owner_dev[:, None] == jnp.arange(owners)[None, :]).astype(jnp.int32)
        slot_rank = jnp.sum((jnp.cumsum(one_hot, axis=0) - one_hot) * one_hot, axis=1)
        slot_index = owner_dev * capacity + slot_rank
        pair_code = ((parents - owner_dev * node_dev) * 2 + rotation).astype(jnp.float32)
        buffer = jnp.zeros((slots_all, states, site_dev), jnp.float32).at[slot_index].set(message)
        code_buffer = jnp.full((slots_all,), -1.0, jnp.float32).at[slot_index].set(pair_code)
        weight_buffer = (
            jnp.zeros((slots_all,), jnp.float32).at[slot_index].set(weights[level_index])
        )
        received, received_codes, received_weights = (
            lax.all_to_all(
                buffer.reshape(owners, capacity, states, site_dev),
                "node",
                split_axis=0,
                concat_axis=0,
                tiled=True,
            ),
            lax.all_to_all(
                code_buffer.reshape(owners, capacity),
                "node",
                split_axis=0,
                concat_axis=0,
                tiled=True,
            ),
            lax.all_to_all(
                weight_buffer.reshape(owners, capacity),
                "node",
                split_axis=0,
                concat_axis=0,
                tiled=True,
            ),
        )
        flat_rows = received.reshape(slots_all, states * site_dev)
        selector = (
            received_codes.reshape(-1).astype(jnp.int32)[None, :]
            == jnp.arange(2 * node_dev)[:, None]
        ).astype(jnp.float32)
        summed = jnp.dot(
            selector * received_weights.reshape(-1)[None, :],
            flat_rows,
            precision=lax.Precision.HIGHEST,
            preferred_element_type=jnp.float32,
        )
        pair_sums = summed.reshape(node_dev, 2, states, site_dev)
        current = pair_sums[:, 0] * pair_sums[:, 1]
    denominator = 0.25 * jnp.sum(current, axis=1)
    node_part = jnp.sum(scaled[None, :] * jnp.log(denominator), axis=1)
    adjoint = pair_sums[:, ::-1] * (scaled[None, :] * 0.25 / denominator)[:, None, None, :]
    adjoint_slots = jnp.dot(
        selector.T,
        adjoint.reshape(2 * node_dev, states * site_dev),
        precision=lax.Precision.HIGHEST,
        preferred_element_type=jnp.float32,
    )
    grad_part = jnp.sum(flat_rows * adjoint_slots, axis=1)
    node_scores, slot_grads = lax.psum((node_part, grad_part), "site")
    own_mult = lax.dynamic_slice_in_dim(multiplicity, device * node_dev, node_dev)
    pair_mult = jnp.repeat(own_mult, 2)
    slot_mult = jnp.dot(
        selector.T, pair_mult, precision=lax.Precision.HIGHEST, preferred_element_type=jnp.float32
    )
    returned = lax.all_to_all(
        (slot_grads * slot_mult).reshape(owners, capacity),
        "node",
        split_axis=0,
        concat_axis=0,
        tiled=True,
    )
    edge_gradient = returned.reshape(-1)[slot_index]
    score_table = lax.all_gather(node_scores, "node", axis=0, tiled=True)
    topology_loglik = jnp.sum(score_table[topo_nodes], axis=1)
    return (topology_loglik, edge_gradient)


def solution(mesh):
    return jax.shard_map(
        on_device,
        mesh=mesh,
        in_specs=(
            P("node", None, "site"),
            P(None, "node", None),
            P(None, "node"),
            P(None, "node"),
            P("site"),
            P("node", None),
        ),
        out_specs=(P("node"), P("node")),
        check_vma=False,
    )
```

profile of v0, /device:TPU:0, one launch (start us, length us, event | category | flops | bytes accessed | tf_op | source)
XLA Modules:
  0.0 903.7 jit_solution(11495351797183941422)
XLA Ops:
  5.4 1.2 scatter_custom_fusion.4
  7.3 10.2 %all-to-all-start.4 = ((f32[64,1,4]{2,1,0:T(1,128)}), f32[64,1,4]{2,1,0:T(1,128)S(1)}, u32[]{:S(2)}, u32[]{:S(2)}) async-start(f32[64,1,4]{2,1,0:T(1,128)} %bitcast.30), calls=%async_computation.4 | async-start | bytes 65536 | tf_op jit(solution)/shard_map/all_to_all | solution.py:52
  18.4 4.1 gather_fusion
  22.5 3.8 reduce_sum.102
  26.4 1.2 scatter_custom_fusion.5
  28.3 10.3 %all-to-all-start.5 = ((f32[64,1,4]{2,1,0:T(1,128)}), f32[64,1,4]{2,1,0:T(1,128)S(1)}, u32[]{:S(2)}, u32[]{:S(2)}) async-start(f32[64,1,4]{2,1,0:T(1,128)} %bitcast.32), calls=%async_computation.5 | async-start | bytes 65536 | tf_op jit(solution)/shard_map/all_to_all | solution.py:59
  38.6 3.8 multiply_add_fusion.2
  42.4 3.0 broadcast.594.clone.1
  45.5 26.2 %scatter_fusion = f32[256,4,1024]{2,1,0:T(4,128)} fusion(f32[256,4,1024]{2,1,0:T(4,128)} %broadcast.594.clone.1, s32[192]{0:T(256)S(1)} %bitcast.186, f32[192,4,1024]{2,1,0:T(4,128)} %multiply_add_fusion.2), kind=kCustom, calls=%fused_computation.11 | custom fusion | bytes 9437952 | tf_op jit(solution)/shard_map/scatter | solution.py:39
  71.6 10.7 %all-to-all-start.6 = ((f32[64,4,4,1024]{3,2,1,0:T(4,128)}), f32[64,4,4,1024]{3,2,1,0:T(4,128)}, u32[]{:S(2)}, u32[]{:S(2)}) async-start(f32[64,4,4,1024]{3,2,1,0:T(4,128)} %bitcast.159), calls=%async_computation.6 | async-start | bytes 8388608 | tf_op jit(solution)/shard_map/all_to_all | solution.py:45
  82.4 1.2 scatter_custom_fusion.2
  87.8 90.8 %all-to-all-done.6 = f32[64,4,4,1024]{3,2,1,0:T(4,128)} async-done(((f32[64,4,4,1024]{3,2,1,0:T(4,128)}), f32[64,4,4,1024]{3,2,1,0:T(4,128)}, u32[]{:S(2)}, u32[]{:S(2)}) %all-to-all-start.6) | async-done | bytes 4194336 | tf_op jit(solution)/shard_map/all_to_all | solution.py:45
  178.6 5.3 all-to-all-start.2
  183.8 8.0 copy.51
  191.8 5.8 copy.35
  197.6 6.6 fusion.4
  205.0 4.1 gather_fusion.1
  209.1 3.8 reduce_sum.103
  213.0 10.3 %all-to-all-start.3 = ((f32[64,1,4]{2,1,0:T(1,128)}), f32[64,1,4]{2,1,0:T(1,128)S(1)}, u32[]{:S(2)}, u32[]{:S(2)}) async-start(f32[64,1,4]{2,1,0:T(1,128)} %bitcast.20), calls=%async_computation.3 | async-start | bytes 65536 | tf_op jit(solution)/shard_map/all_to_all | solution.py:59
  223.3 3.8 multiply_add_fusion.1
  227.1 3.0 broadcast.594.clone
  230.1 26.2 %scatter_fusion.1 = f32[256,4,1024]{2,1,0:T(4,128)} fusion(f32[256,4,1024]{2,1,0:T(4,128)} %broadcast.594.clone, s32[192]{0:T(256)S(1)} %bitcast.182, f32[192,4,1024]{2,1,0:T(4,128)} %multiply_add_fusion.1), kind=kCustom, calls=%fused_computation.12 | custom fusion | bytes 9437952 | tf_op jit(solution)/shard_map/scatter | solution.py:39
  256.3 10.9 %all-to-all-start.7 = ((f32[64,4,4,1024]{3,2,1,0:T(4,128)}), f32[64,4,4,1024]{3,2,1,0:T(4,128)}, u32[]{:S(2)}, u32[]{:S(2)}) async-start(f32[64,4,4,1024]{3,2,1,0:T(4,128)} %bitcast.160), calls=%async_computation.7 | async-start | bytes 8388608 | tf_op jit(solution)/shard_map/all_to_all | solution.py:45
  267.3 1.2 scatter_custom_fusion
  272.2 91.3 %all-to-all-done.7 = f32[64,4,4,1024]{3,2,1,0:T(4,128)} async-done(((f32[64,4,4,1024]{3,2,1,0:T(4,128)}), f32[64,4,4,1024]{3,2,1,0:T(4,128)}, u32[]{:S(2)}, u32[]{:S(2)}) %all-to-all-start.7) | async-done | bytes 4194336 | tf_op jit(solution)/shard_map/all_to_all | solution.py:45
  363.5 5.3 all-to-all-start
  368.7 8.0 copy.52
  376.7 5.7 copy.37
  382.4 6.6 fusion.6
  389.9 4.1 gather_fusion.2
  393.9 3.8 reduce_sum.104
  397.9 10.3 %all-to-all-start.1 = ((f32[64,1,4]{2,1,0:T(1,128)}), f32[64,1,4]{2,1,0:T(1,128)S(1)}, u32[]{:S(2)}, u32[]{:S(2)}) async-start(f32[64,1,4]{2,1,0:T(1,128)} %bitcast.8), calls=%async_computation.1 | async-start | bytes 65536 | tf_op jit(solution)/shard_map/all_to_all | solution.py:59
  408.2 3.8 multiply_add_fusion
  412.0 3.0 broadcast.594
  415.0 26.2 %scatter_fusion.2 = f32[256,4,1024]{2,1,0:T(4,128)} fusion(f32[256,4,1024]{2,1,0:T(4,128)} %broadcast.594, s32[192]{0:T(256)S(1)} %bitcast.171, f32[192,4,1024]{2,1,0:T(4,128)} %multiply_add_fusion), kind=kCustom, calls=%fused_computation.13 | custom fusion | bytes 9437952 | tf_op jit(solution)/shard_map/scatter | solution.py:39
  441.2 10.7 %all-to-all-start.8 = ((f32[64,4,4,1024]{3,2,1,0:T(4,128)}), f32[64,4,4,1024]{3,2,1,0:T(4,128)}, u32[]{:S(2)}, u32[]{:S(2)}) async-start(f32[64,4,4,1024]{3,2,1,0:T(4,128)} %bitcast.161), calls=%async_computation.8 | async-start | bytes 8388608 | tf_op jit(solution)/shard_map/all_to_all | solution.py:45
  451.9 135.2 %all-gather = s32[64,4,8]{2,1,0:T(4,128)S(1)} all-gather(s32[1,4,8]{2,1,0:T(4,128)S(1)} %bitcast.179), channel_id=1, replica_groups=mesh['node'=64,'site'=4] {'node'}, dimensions={0}, use_global_device_ids=true | all-gather | bytes 8320 | tf_op jit(solution)/shard_map/all_gather | solution.py:22
  587.3 11.2 %scatter_custom_fusion.9 = f32[4096]{0:T(1024)S(1)} fusion(s32[2048]{0:T(1024)S(1)} %reshape.800, f32[2048]{0:T(1024)S(1)} %broadcast.600, f32[]{:T(128)} %constant.79.clone.1), kind=kCustom, calls=%fused_computation.94 | custom fusion | flops 2048 | bytes 16388 | tf_op jit(solution)/shard_map/scatter-add | solution.py:23
  601.5 8.0 copy.53
  609.4 5.6 copy.39
  615.0 6.6 fusion.8
  622.3 1.4 copy.40
  623.6 1.7 copy.54
  625.8 2.4 fusion
  628.2 10.7 %all-reduce.4 = (f32[64]{0:T(128)S(1)}, f32[256]{0:T(256)S(1)}) all-reduce(f32[64]{0:T(128)S(1)} %get-tuple-element.11, f32[256]{0:T(256)S(1)} %fusion), channel_id=1, replica_groups=mesh['node'=64,'site'=4] {'site'}, use_global_device_ids=true, to_apply=%region_23.24 | all-reduce | flops 320 | bytes 2560 | tf_op jit(solution)/shard_map/psum | solution.py:90
  639.7 7.9 all-to-all-start.9
  647.8 251.0 %all-reduce.3 = f32[4096]{0:T(1024)S(1)} all-reduce(f32[4096]{0:T(1024)S(1)} %dynamic-update-slice), channel_id=1, replica_groups=mesh['node'=64,'site'=4] {'node'}, use_global_device_ids=true, to_apply=%add.3 | all-reduce | flops 4096 | bytes 32768
  901.1 2.2 gather_fusion.4
  (112 shorter events, 23.5 us)
Async XLA Ops:
  0.6 17.8 %copy-start = (f32[64,4,1024]{2,1,0:T(4,128)S(1)}, f32[64,4,1024]{2,1,0:T(4,128)}, u32[]{:S(2)}) copy-start(f32[64,4,1024]{2,1,0:T(4,128)} %param.6) | copy-start | bytes 3145732
  7.3 21.0 %all-to-all-start.4 = ((f32[64,1,4]{2,1,0:T(1,128)}), f32[64,1,4]{2,1,0:T(1,128)S(1)}, u32[]{:S(2)}, u32[]{:S(2)}) async-start(f32[64,1,4]{2,1,0:T(1,128)} %bitcast.30), calls=%async_computation.4 | async-start | bytes 65536 | tf_op jit(solution)/shard_map/all_to_all | solution.py:52
  22.5 3.9 copy-start.5
  28.3 43.3 %all-to-all-start.5 = ((f32[64,1,4]{2,1,0:T(1,128)}), f32[64,1,4]{2,1,0:T(1,128)S(1)}, u32[]{:S(2)}, u32[]{:S(2)}) async-start(f32[64,1,4]{2,1,0:T(1,128)} %bitcast.32), calls=%async_computation.5 | async-start | bytes 65536 | tf_op jit(solution)/shard_map/all_to_all | solution.py:59
  71.6 107.0 %all-to-all-start.6 = ((f32[64,4,4,1024]{3,2,1,0:T(4,128)}), f32[64,4,4,1024]{3,2,1,0:T(4,128)}, u32[]{:S(2)}, u32[]{:S(2)}) async-start(f32[64,4,4,1024]{3,2,1,0:T(4,128)} %bitcast.159), calls=%async_computation.6 | async-start | bytes 8388608 | tf_op jit(solution)/shard_map/all_to_all | solution.py:45
  178.6 34.4 %all-to-all-start.2 = ((f32[64,1,4]{2,1,0:T(1,128)}), f32[64,1,4]{2,1,0:T(1,128)S(1)}, u32[]{:S(2)}, u32[]{:S(2)}) async-start(f32[64,1,4]{2,1,0:T(1,128)} %bitcast.18), calls=%async_computation.2 | async-start | bytes 65536 | tf_op jit(solution)/shard_map/all_to_all | solution.py:52
  213.0 43.3 %all-to-all-start.3 = ((f32[64,1,4]{2,1,0:T(1,128)}), f32[64,1,4]{2,1,0:T(1,128)S(1)}, u32[]{:S(2)}, u32[]{:S(2)}) async-start(f32[64,1,4]{2,1,0:T(1,128)} %bitcast.20), calls=%async_computation.3 | async-start | bytes 65536 | tf_op jit(solution)/shard_map/all_to_all | solution.py:59
  256.3 107.1 %all-to-all-start.7 = ((f32[64,4,4,1024]{3,2,1,0:T(4,128)}), f32[64,4,4,1024]{3,2,1,0:T(4,128)}, u32[]{:S(2)}, u32[]{:S(2)}) async-start(f32[64,4,4,1024]{3,2,1,0:T(4,128)} %bitcast.160), calls=%async_computation.7 | async-start | bytes 8388608 | tf_op jit(solution)/shard_map/all_to_all | solution.py:45
  363.5 34.4 %all-to-all-start = ((f32[64,1,4]{2,1,0:T(1,128)}), f32[64,1,4]{2,1,0:T(1,128)S(1)}, u32[]{:S(2)}, u32[]{:S(2)}) async-start(f32[64,1,4]{2,1,0:T(1,128)} %bitcast.6), calls=%async_computation | async-start | bytes 65536 | tf_op jit(solution)/shard_map/all_to_all | solution.py:52
  397.9 43.3 %all-to-all-start.1 = ((f32[64,1,4]{2,1,0:T(1,128)}), f32[64,1,4]{2,1,0:T(1,128)S(1)}, u32[]{:S(2)}, u32[]{:S(2)}) async-start(f32[64,1,4]{2,1,0:T(1,128)} %bitcast.8), calls=%async_computation.1 | async-start | bytes 65536 | tf_op jit(solution)/shard_map/all_to_all | solution.py:59
  441.2 10.7 %copy-start.3 = (s32[4,8]{1,0:T(4,128)S(1)}, s32[4,8]{1,0:T(4,128)}, u32[]{:S(2)}) copy-start(s32[4,8]{1,0:T(4,128)} %param.11) | copy-start | bytes 388
  441.2 157.7 %copy-start.6 = (u32[256]{0:T(256)S(1)}, u32[256]{0:T(256)}, u32[]{:S(2)}) copy-start(u32[256]{0:T(256)} %constant.96) | copy-start | bytes 3076
  441.2 159.0 %copy-start.4 = (s32[1024]{0:T(1024)S(1)}, s32[1024]{0:T(1024)}, u32[]{:S(2)}) copy-start(s32[1024]{0:T(1024)} %param.10) | copy-start | bytes 12292
  441.2 160.3 %all-to-all-start.8 = ((f32[64,4,4,1024]{3,2,1,0:T(4,128)}), f32[64,4,4,1024]{3,2,1,0:T(4,128)}, u32[]{:S(2)}, u32[]{:S(2)}) async-start(f32[64,4,4,1024]{3,2,1,0:T(4,128)} %bitcast.161), calls=%async_computation.8 | async-start | bytes 8388608 | tf_op jit(solution)/shard_map/all_to_all | solution.py:45
  623.6 2.2 copy-start.2
  625.8 277.5 %copy-start.1 = (f32[64,4,1024]{2,1,0:T(4,128)S(1)}, f32[64,4,1024]{2,1,0:T(4,128)}, u32[]{:S(2)}) copy-start(f32[64,4,1024]{2,1,0:T(4,128)} %param.6) | copy-start | bytes 3145732
  639.7 260.6 %all-to-all-start.9 = ((f32[64,1,4]{2,1,0:T(1,128)}), f32[64,1,4]{2,1,0:T(1,128)S(1)}, u32[]{:S(2)}, u32[]{:S(2)}) async-start(f32[64,1,4]{2,1,0:T(1,128)} %bitcast.59), calls=%async_computation.9 | async-start | bytes 65536 | tf_op jit(solution)/shard_map/all_to_all | solution.py:96
where the time goes:
time: 914 us; the launch traced here: 904 us
  blocking collectives  397 us (43%)
  waiting for transfers between devices  182 us (20%)
  local copies, waits for them, and re-layouts  165 us (18%)
  starting transfers between devices  91.8 us (10%)
  other arithmetic  43.2 us (5%)
  matrix products  22.3 us (2%)
    unnamed x1, blocking collectives  251 us
    all_to_all x3, waiting for transfers between devices, on_device(): lax.all_to_all(buffer.reshape(owners, capacity, states, site_dev), 'node'...  182 us
    all_gather x1, blocking collectives, on_device(): incidence = lax.all_gather(topo_nodes, 'node', axis=0, tiled=True)  135 us
    scatter x3, local copies, waits for them, and re-layouts, on_device(): jnp.zeros((slots_all, states, site_dev), jnp.float32).at[slot_index]  78.5 us
    all_to_all x3, starting transfers between devices, on_device(): lax.all_to_all(buffer.reshape(owners, capacity, states, site_dev), 'node'...  32.3 us
    all_to_all x3, starting transfers between devices, on_device(): lax.all_to_all(weight_buffer.reshape(owners, capacity), 'node', split_axi...  30.9 us
    unnamed x21, local copies, waits for them, and re-layouts  26.9 us
    all_to_all x3, starting transfers between devices, on_device(): lax.all_to_all(code_buffer.reshape(owners, capacity), 'node', split_axis=...  20.7 us
  transfers between devices with their start and end apart: 10, of which 2 were waited for; matrix products, arithmetic and copies ran while one was open for 21% of the time, Pallas kernels for 0%

commit v1 on v0

--- a/solution.py
+++ b/solution.py
@@ -2,6 +2,13 @@
 import jax.numpy as jnp
 from jax import lax
 from jax.sharding import PartitionSpec as P
+
+
+def exchange_gather(x, axis, dim):
+    size = lax.axis_size(axis)
+    tiles = jnp.stack([x for _ in range(size)])
+    tiles = lax.all_to_all(tiles, axis, split_axis=0, concat_axis=0)
+    return jnp.concatenate(tiles, axis=dim)
 
 
 def transit(child_rows, branch):
@@ -19,7 +26,7 @@
     nodes_all = node_dev * owners
     sites_all = site_dev * lax.axis_size("site")
     scaled = counts.astype(jnp.float32) / sites_all
-    incidence = lax.all_gather(topo_nodes, "node", axis=0, tiled=True)
+    incidence = exchange_gather(topo_nodes, "node", 0)
     multiplicity = jax.ops.segment_sum(
         jnp.ones((incidence.size,), jnp.float32), incidence.reshape(-1), num_segments=nodes_all
     )

time: 914 us -> 873 us (0.955)
  blocking collectives: 397 us -> 262 us
  waiting for transfers between devices: 182 us -> 273 us
    all_gather x1 -> x0, blocking collectives: 135 us -> none  [on_device(): incidence = lax.all_gather(topo_nodes, 'node', axis=0, tiled=True)]
    all_to_all x3, waiting for transfers between devices: 182 us -> 264 us  [on_device(): lax.all_to_all(buffer.reshape(owners, capacity, states, site_dev), 'node'...]
    all_to_all x3, waiting for transfers between devices: 0.01 us -> 9.48 us  [on_device(): lax.all_to_all(weight_buffer.reshape(owners, capacity), 'node', split_axi...]
  transfers between devices with their start and end apart: 10 -> 11, of which waited for: 2 -> 4; matrix products, arithmetic and copies ran while one was open for 21% -> 22% of each run, Pallas kernels for 0% -> 0%
where the time goes in v1:
time: 873 us; the launch traced here: 863 us
  waiting for transfers between devices  273 us (31%)
  blocking collectives  262 us (30%)
  local copies, waits for them, and re-layouts  166 us (19%)
  starting transfers between devices  94 us (11%)
  other arithmetic  43.2 us (5%)
  matrix products  22.3 us (3%)
    all_to_all x3, waiting for transfers between devices, on_device(): lax.all_to_all(buffer.reshape(owners, capacity, states, site_dev), 'node'...  264 us
    unnamed x1, blocking collectives  251 us
    scatter x3, local copies, waits for them, and re-layouts, on_device(): jnp.zeros((slots_all, states, site_dev), jnp.float32).at[slot_index]  78.5 us
    all_to_all x3, starting transfers between devices, on_device(): lax.all_to_all(buffer.reshape(owners, capacity, states, site_dev), 'node'...  32.6 us
    all_to_all x3, starting transfers between devices, on_device(): lax.all_to_all(weight_buffer.reshape(owners, capacity), 'node', split_axi...  30.9 us
    unnamed x21, local copies, waits for them, and re-layouts  26.9 us
    all_to_all x3, starting transfers between devices, on_device(): lax.all_to_all(code_buffer.reshape(owners, capacity), 'node', split_axis=...  20.7 us
    dot_general x3, matrix products, on_device(): jnp.dot(selector * received_weights.reshape(-1)[None, :], flat_rows, prec...  19.7 us
  transfers between devices with their start and end apart: 11, of which 4 were waited for; matrix products, arithmetic and copies ran while one was open for 22% of the time, Pallas kernels for 0%

profile of v1, /device:TPU:0, one launch (start us, length us, event | category | flops | bytes accessed | tf_op | source)
XLA Modules:
  0.0 862.6 jit_solution(13500582443958763485)
XLA Ops:
  5.4 1.2 scatter_custom_fusion.4
  7.3 10.2 %all-to-all-start.4 = ((f32[64,1,4]{2,1,0:T(1,128)}), f32[64,1,4]{2,1,0:T(1,128)S(1)}, u32[]{:S(2)}, u32[]{:S(2)}) async-start(f32[64,1,4]{2,1,0:T(1,128)} %bitcast.30), calls=%async_computation.4 | async-start | bytes 65536 | tf_op jit(solution)/shard_map/all_to_all | solution.py:59
  18.4 4.1 gather_fusion
  22.5 3.8 reduce_sum.102
  26.4 1.2 scatter_custom_fusion.5
  28.3 10.3 %all-to-all-start.5 = ((f32[64,1,4]{2,1,0:T(1,128)}), f32[64,1,4]{2,1,0:T(1,128)S(1)}, u32[]{:S(2)}, u32[]{:S(2)}) async-start(f32[64,1,4]{2,1,0:T(1,128)} %bitcast.32), calls=%async_computation.5 | async-start | bytes 65536 | tf_op jit(solution)/shard_map/all_to_all | solution.py:66
  38.6 3.8 multiply_add_fusion.2
  42.4 3.0 broadcast.596.clone.1
  45.5 26.2 %scatter_fusion = f32[256,4,1024]{2,1,0:T(4,128)} fusion(f32[256,4,1024]{2,1,0:T(4,128)} %broadcast.596.clone.1, s32[192]{0:T(256)S(1)} %bitcast.184, f32[192,4,1024]{2,1,0:T(4,128)} %multiply_add_fusion.2), kind=kCustom, calls=%fused_computation.11 | custom fusion | bytes 9437952 | tf_op jit(solution)/shard_map/scatter | solution.py:46
  71.6 10.7 %all-to-all-start.6 = ((f32[64,4,4,1024]{3,2,1,0:T(4,128)}), f32[64,4,4,1024]{3,2,1,0:T(4,128)}, u32[]{:S(2)}, u32[]{:S(2)}) async-start(f32[64,4,4,1024]{3,2,1,0:T(4,128)} %bitcast.158), calls=%async_computation.6 | async-start | bytes 8388608 | tf_op jit(solution)/shard_map/all_to_all | solution.py:52
  87.8 90.8 %all-to-all-done.6 = f32[64,4,4,1024]{3,2,1,0:T(4,128)} async-done(((f32[64,4,4,1024]{3,2,1,0:T(4,128)}), f32[64,4,4,1024]{3,2,1,0:T(4,128)}, u32[]{:S(2)}, u32[]{:S(2)}) %all-to-all-start.6) | async-done | bytes 4194336 | tf_op jit(solution)/shard_map/all_to_all | solution.py:52
  178.6 5.3 all-to-all-start.2
  183.8 8.0 copy.51
  191.8 5.8 copy.35
  197.6 6.6 fusion.4
  205.0 4.1 gather_fusion.1
  209.1 3.8 reduce_sum.103
  213.0 10.3 %all-to-all-start.3 = ((f32[64,1,4]{2,1,0:T(1,128)}), f32[64,1,4]{2,1,0:T(1,128)S(1)}, u32[]{:S(2)}, u32[]{:S(2)}) async-start(f32[64,1,4]{2,1,0:T(1,128)} %bitcast.20), calls=%async_computation.3 | async-start | bytes 65536 | tf_op jit(solution)/shard_map/all_to_all | solution.py:66
  223.3 3.8 multiply_add_fusion.1
  227.1 3.0 broadcast.596.clone
  230.1 26.2 %scatter_fusion.1 = f32[256,4,1024]{2,1,0:T(4,128)} fusion(f32[256,4,1024]{2,1,0:T(4,128)} %broadcast.596.clone, s32[192]{0:T(256)S(1)} %bitcast.180, f32[192,4,1024]{2,1,0:T(4,128)} %multiply_add_fusion.1), kind=kCustom, calls=%fused_computation.12 | custom fusion | bytes 9437952 | tf_op jit(solution)/shard_map/scatter | solution.py:46
  256.3 10.9 %all-to-all-start.7 = ((f32[64,4,4,1024]{3,2,1,0:T(4,128)}), f32[64,4,4,1024]{3,2,1,0:T(4,128)}, u32[]{:S(2)}, u32[]{:S(2)}) async-start(f32[64,4,4,1024]{3,2,1,0:T(4,128)} %bitcast.159), calls=%async_computation.7 | async-start | bytes 8388608 | tf_op jit(solution)/shard_map/all_to_all | solution.py:52
  272.2 91.3 %all-to-all-done.7 = f32[64,4,4,1024]{3,2,1,0:T(4,128)} async-done(((f32[64,4,4,1024]{3,2,1,0:T(4,128)}), f32[64,4,4,1024]{3,2,1,0:T(4,128)}, u32[]{:S(2)}, u32[]{:S(2)}) %all-to-all-start.7) | async-done | bytes 4194336 | tf_op jit(solution)/shard_map/all_to_all | solution.py:52
  363.5 5.3 all-to-all-start
  368.7 8.0 copy.52
  376.7 5.7 copy.37
  382.4 6.6 fusion.6
  389.9 4.1 gather_fusion.2
  394.0 3.8 reduce_sum.104
  397.8 10.3 %all-to-all-start.1 = ((f32[64,1,4]{2,1,0:T(1,128)}), f32[64,1,4]{2,1,0:T(1,128)S(1)}, u32[]{:S(2)}, u32[]{:S(2)}) async-start(f32[64,1,4]{2,1,0:T(1,128)} %bitcast.8), calls=%async_computation.1 | async-start | bytes 65536 | tf_op jit(solution)/shard_map/all_to_all | solution.py:66
  408.2 9.5 %all-to-all-done.1 = f32[64,1,4]{2,1,0:T(1,128)S(1)} async-done(((f32[64,1,4]{2,1,0:T(1,128)}), f32[64,1,4]{2,1,0:T(1,128)S(1)}, u32[]{:S(2)}, u32[]{:S(2)}) %all-to-all-start.1) | async-done | bytes 1056 | tf_op jit(solution)/shard_map/all_to_all | solution.py:66
  418.4 4.6 all-to-all-start.9
  423.0 3.8 multiply_add_fusion
  426.8 3.0 broadcast.596
  429.8 26.2 %scatter_fusion.2 = f32[256,4,1024]{2,1,0:T(4,128)} fusion(f32[256,4,1024]{2,1,0:T(4,128)} %broadcast.596, s32[192]{0:T(256)S(1)} %bitcast.170, f32[192,4,1024]{2,1,0:T(4,128)} %multiply_add_fusion), kind=kCustom, calls=%fused_computation.13 | custom fusion | bytes 9437952 | tf_op jit(solution)/shard_map/scatter | solution.py:46
  456.0 10.9 %all-to-all-start.8 = ((f32[64,4,4,1024]{3,2,1,0:T(4,128)}), f32[64,4,4,1024]{3,2,1,0:T(4,128)}, u32[]{:S(2)}, u32[]{:S(2)}) async-start(f32[64,4,4,1024]{3,2,1,0:T(4,128)} %bitcast.160), calls=%async_computation.8 | async-start | bytes 8388608 | tf_op jit(solution)/shard_map/all_to_all | solution.py:52
  469.5 11.2 %scatter_custom_fusion.9 = f32[4096]{0:T(1024)S(1)} fusion(s32[2048]{0:T(1024)S(1)} %reshape.802, f32[2048]{0:T(1024)S(1)} %broadcast.602, f32[]{:T(128)} %constant.79.clone.1), kind=kCustom, calls=%fused_computation.94 | custom fusion | flops 2048 | bytes 16388 | tf_op jit(solution)/shard_map/scatter-add | solution.py:30
  481.2 81.9 %all-to-all-done.8 = f32[64,4,4,1024]{3,2,1,0:T(4,128)} async-done(((f32[64,4,4,1024]{3,2,1,0:T(4,128)}), f32[64,4,4,1024]{3,2,1,0:T(4,128)}, u32[]{:S(2)}, u32[]{:S(2)}) %all-to-all-start.8) | async-done | bytes 4194336 | tf_op jit(solution)/shard_map/all_to_all | solution.py:52
  563.1 7.9 copy.53
  571.0 5.6 copy.39
  576.6 6.6 fusion.8
  583.8 1.4 copy.40
  585.2 1.7 copy.54
  587.4 2.4 fusion
  589.8 10.7 %all-reduce.4 = (f32[64]{0:T(128)S(1)}, f32[256]{0:T(256)S(1)}) all-reduce(f32[64]{0:T(128)S(1)} %get-tuple-element.11, f32[256]{0:T(256)S(1)} %fusion), channel_id=1, replica_groups=mesh['node'=64,'site'=4] {'site'}, use_global_device_ids=true, to_apply=%region_23.24 | all-reduce | flops 320 | bytes 2560 | tf_op jit(solution)/shard_map/psum | solution.py:97
  601.3 5.2 all-to-all-start.10
  606.8 251.0 %all-reduce.3 = f32[4096]{0:T(1024)S(1)} all-reduce(f32[4096]{0:T(1024)S(1)} %dynamic-update-slice), channel_id=1, replica_groups=mesh['node'=64,'site'=4] {'node'}, use_global_device_ids=true, to_apply=%add.3 | all-reduce | flops 4096 | bytes 32768
  860.1 2.2 gather_fusion.4
  (114 shorter events, 26.6 us)
Async XLA Ops:
  0.6 17.8 %copy-start = (f32[64,4,1024]{2,1,0:T(4,128)S(1)}, f32[64,4,1024]{2,1,0:T(4,128)}, u32[]{:S(2)}) copy-start(f32[64,4,1024]{2,1,0:T(4,128)} %param.6) | copy-start | bytes 3145732
  7.3 21.0 %all-to-all-start.4 = ((f32[64,1,4]{2,1,0:T(1,128)}), f32[64,1,4]{2,1,0:T(1,128)S(1)}, u32[]{:S(2)}, u32[]{:S(2)}) async-start(f32[64,1,4]{2,1,0:T(1,128)} %bitcast.30), calls=%async_computation.4 | async-start | bytes 65536 | tf_op jit(solution)/shard_map/all_to_all | solution.py:59
  22.5 3.9 copy-start.5
  28.3 43.3 %all-to-all-start.5 = ((f32[64,1,4]{2,1,0:T(1,128)}), f32[64,1,4]{2,1,0:T(1,128)S(1)}, u32[]{:S(2)}, u32[]{:S(2)}) async-start(f32[64,1,4]{2,1,0:T(1,128)} %bitcast.32), calls=%async_computation.5 | async-start | bytes 65536 | tf_op jit(solution)/shard_map/all_to_all | solution.py:66
  71.6 107.0 %all-to-all-start.6 = ((f32[64,4,4,1024]{3,2,1,0:T(4,128)}), f32[64,4,4,1024]{3,2,1,0:T(4,128)}, u32[]{:S(2)}, u32[]{:S(2)}) async-start(f32[64,4,4,1024]{3,2,1,0:T(4,128)} %bitcast.158), calls=%async_computation.6 | async-start | bytes 8388608 | tf_op jit(solution)/shard_map/all_to_all | solution.py:52
  178.6 34.4 %all-to-all-start.2 = ((f32[64,1,4]{2,1,0:T(1,128)}), f32[64,1,4]{2,1,0:T(1,128)S(1)}, u32[]{:S(2)}, u32[]{:S(2)}) async-start(f32[64,1,4]{2,1,0:T(1,128)} %bitcast.18), calls=%async_computation.2 | async-start | bytes 65536 | tf_op jit(solution)/shard_map/all_to_all | solution.py:59
  213.0 43.3 %all-to-all-start.3 = ((f32[64,1,4]{2,1,0:T(1,128)}), f32[64,1,4]{2,1,0:T(1,128)S(1)}, u32[]{:S(2)}, u32[]{:S(2)}) async-start(f32[64,1,4]{2,1,0:T(1,128)} %bitcast.20), calls=%async_computation.3 | async-start | bytes 65536 | tf_op jit(solution)/shard_map/all_to_all | solution.py:66
  256.3 107.1 %all-to-all-start.7 = ((f32[64,4,4,1024]{3,2,1,0:T(4,128)}), f32[64,4,4,1024]{3,2,1,0:T(4,128)}, u32[]{:S(2)}, u32[]{:S(2)}) async-start(f32[64,4,4,1024]{3,2,1,0:T(4,128)} %bitcast.159), calls=%async_computation.7 | async-start | bytes 8388608 | tf_op jit(solution)/shard_map/all_to_all | solution.py:52
  363.5 34.3 %all-to-all-start = ((f32[64,1,4]{2,1,0:T(1,128)}), f32[64,1,4]{2,1,0:T(1,128)S(1)}, u32[]{:S(2)}, u32[]{:S(2)}) async-start(f32[64,1,4]{2,1,0:T(1,128)} %bitcast.6), calls=%async_computation | async-start | bytes 65536 | tf_op jit(solution)/shard_map/all_to_all | solution.py:59
  393.9 23.7 %copy-start.3 = (s32[4,8]{1,0:T(4,128)S(1)}, s32[4,8]{1,0:T(4,128)}, u32[]{:S(2)}) copy-start(s32[4,8]{1,0:T(4,128)} %param.11) | copy-start | bytes 388
  397.8 19.9 %all-to-all-start.1 = ((f32[64,1,4]{2,1,0:T(1,128)}), f32[64,1,4]{2,1,0:T(1,128)S(1)}, u32[]{:S(2)}, u32[]{:S(2)}) async-start(f32[64,1,4]{2,1,0:T(1,128)} %bitcast.8), calls=%async_computation.1 | async-start | bytes 65536 | tf_op jit(solution)/shard_map/all_to_all | solution.py:66
  418.4 37.6 %all-to-all-start.9 = ((s32[64,4,8]{2,1,0:T(4,128)}), s32[64,4,8]{2,1,0:T(4,128)S(1)}, u32[]{:S(2)}, u32[]{:S(2)}) async-start(s32[64,4,8]{2,1,0:T(4,128)} %stack.2), calls=%async_computation.9 | async-start | bytes 262144 | tf_op jit(solution)/shard_map/all_to_all | solution.py:10
  456.0 11.0 %copy-start.6 = (u32[256]{0:T(256)S(1)}, u32[256]{0:T(256)}, u32[]{:S(2)}) copy-start(u32[256]{0:T(256)} %constant.96) | copy-start | bytes 3076
  456.0 12.3 %copy-start.4 = (s32[1024]{0:T(1024)S(1)}, s32[1024]{0:T(1024)}, u32[]{:S(2)}) copy-start(s32[1024]{0:T(1024)} %param.10) | copy-start | bytes 12292
  456.0 107.1 %all-to-all-start.8 = ((f32[64,4,4,1024]{3,2,1,0:T(4,128)}), f32[64,4,4,1024]{3,2,1,0:T(4,128)}, u32[]{:S(2)}, u32[]{:S(2)}) async-start(f32[64,4,4,1024]{3,2,1,0:T(4,128)} %bitcast.160), calls=%async_computation.8 | async-start | bytes 8388608 | tf_op jit(solution)/shard_map/all_to_all | solution.py:52
  585.2 2.2 copy-start.2
  587.4 274.9 %copy-start.1 = (f32[64,4,1024]{2,1,0:T(4,128)S(1)}, f32[64,4,1024]{2,1,0:T(4,128)}, u32[]{:S(2)}) copy-start(f32[64,4,1024]{2,1,0:T(4,128)} %param.6) | copy-start | bytes 3145732
  601.3 258.0 %all-to-all-start.10 = ((f32[64,1,4]{2,1,0:T(1,128)}), f32[64,1,4]{2,1,0:T(1,128)S(1)}, u32[]{:S(2)}, u32[]{:S(2)}) async-start(f32[64,1,4]{2,1,0:T(1,128)} %bitcast.58), calls=%async_computation.10 | async-start | bytes 65536 | tf_op jit(solution)/shard_map/all_to_all | solution.py:103
